TPU v7x, 128 devices: a whole 4x4x4 slice. The times are simulated.
128 devices in a mesh: tiles: 16 (over y, x), gauss: 8 (over z, core).
Axes of the slice: x: 4, y: 4, z: 4, core: 2. Of those that a mesh axis runs over, the one named last changes fastest.
Arguments:
- params: float32 [59, 2097152], P(None, ('tiles', 'gauss')), may hold values from -9 to 4.5, as said below
- adam_m: float32 [59, 2097152], P(None, ('tiles', 'gauss')), may hold values from -0.03 to 0.03
- adam_v: float32 [59, 2097152], P(None, ('tiles', 'gauss')), may hold values from 0.05 to 2
- cameras: float32 [4, 13], replicated, may hold values from -0.5 to 2000, as said below
- exposure: float32 [4, 3], replicated, may hold values from 0.5 to 1.5
- entry_owner: int32 [512, 1024], P(('tiles', 'gauss')), may hold values from 0 to 127, as said below
- entry_local: int32 [512, 1024], P(('tiles', 'gauss')), may hold values from 0 to 16383
- block_counts: int32 [512], P(('tiles', 'gauss')), may hold values from 2 to 4, as said below
- tile_view: int32 [512], P(('tiles', 'gauss')), may hold values from 0 to 3
- tile_spot: int32 [512], P(('tiles', 'gauss')), may hold values from 12580 to 19579
- d_image: float32 [512, 3, 256], P(('tiles', 'gauss')), may hold values from -320 to 320
Outputs:
- new_params: float32 [59, 2097152], P(None, ('tiles', 'gauss'))
- new_m: float32 [59, 2097152], P(None, ('tiles', 'gauss'))
- new_v: float32 [59, 2097152], P(None, ('tiles', 'gauss'))
- exposure_grad: float32 [4, 3], replicated
Inputs may be any that keep to these rules, and one draw needn't show every extreme that they name: `params`: components 0 to 2 lie in -4.5 to 4.5, components 3 to 5 in -5 to -2, component 6 in 0.5 to 1.5, component 10 in -9 to -7.5. `cameras`: each row holds a matrix whose entries differ from the identity's by at most 0.1, a translation with first two entries in -0.5 to 0.5 and third in 5 to 6, and a focal length in 1400 to 2000. `entry_owner`: of the 4096 entries of one device's lists (rendered or not), at most 48 name any one owner; in every draw one owner is named exactly 48 times by every device. `block_counts`: every device holds a tile of 4 blocks.
All inputs are finite; a program needn't handle non-finite values.
Results may differ from a plain program's by a relative error of at most 0.0003.
Values sent between devices are 32-bit elements; how exact they have to be, the bound alone decides.
No kernel may reach another device: no remote copies, remote signals or barrier semaphores. Data moves between devices by JAX's collectives and lax.ppermute only.
A program may use at most 256 MiB of HBM per device.

v0:
```python
import jax
import jax.numpy as jnp
from jax import lax
from jax.sharding import PartitionSpec as P

VIEWS = 4
BLOCK = 256
TILE = 16
IMG_W = 3840
IMG_H = 2160
PARAMS = 59
TPIX = 256
sh_c0 = 0.28209479177387814
sh_c1 = 0.4886025119029199
sh_c2 = (
    1.0925484305920792,
    -1.0925484305920792,
    0.31539156525252005,
    -1.0925484305920792,
    0.5462742152960396,
)
sh_c3 = (
    -0.5900435899266435,
    2.890611442640554,
    -0.4570457994644658,
    0.3731763325901154,
    -0.4570457994644658,
    1.445305721320277,
    -0.5900435899266435,
)
beta_first = 0.9
beta_second = 0.999
learn_rate = 0.01
adam_eps = 1e-08
fix_first = 1.0
fix_second = 0.632304575229036
blur_add = 0.3


def sh_color(values, unit_x, unit_y, unit_z):
    coefficients = [values[11 + 3 * index_k : 14 + 3 * index_k] for index_k in range(16)]
    square_x = unit_x * unit_x
    square_y = unit_y * unit_y
    square_z = unit_z * unit_z
    basis_list = [
        -sh_c1 * unit_y,
        sh_c1 * unit_z,
        -sh_c1 * unit_x,
        sh_c2[0] * unit_x * unit_y,
        sh_c2[1] * unit_y * unit_z,
        sh_c2[2] * (2.0 * square_z - square_x - square_y),
        sh_c2[3] * unit_x * unit_z,
        sh_c2[4] * (square_x - square_y),
        sh_c3[0] * unit_y * (3.0 * square_x - square_y),
        sh_c3[1] * unit_x * unit_y * unit_z,
        sh_c3[2] * unit_y * (4.0 * square_z - square_x - square_y),
        sh_c3[3] * unit_z * (2.0 * square_z - 3.0 * square_x - 3.0 * square_y),
        sh_c3[4] * unit_x * (4.0 * square_z - square_x - square_y),
        sh_c3[5] * unit_z * (square_x - square_y),
        sh_c3[6] * unit_x * (square_x - 3.0 * square_y),
    ]
    summed = 0.5 + sh_c0 * coefficients[0]
    for index_k in range(15):
        summed = summed + basis_list[index_k] * coefficients[index_k + 1]
    return jnp.maximum(summed, 0.0)


def project(values, camera):
    points = [values[0], values[1], values[2]]
    matrix = [[camera[3 * row_at + col_at] for col_at in range(3)] for row_at in range(3)]
    translation = [camera[9], camera[10], camera[11]]
    focal_len = camera[12]
    viewed = [
        matrix[row_at][0] * points[0]
        + matrix[row_at][1] * points[1]
        + matrix[row_at][2] * points[2]
        + translation[row_at]
        for row_at in range(3)
    ]
    inverse_depth = 1.0 / viewed[2]
    screen_x = focal_len * viewed[0] * inverse_depth + 0.5 * IMG_W
    screen_y = focal_len * viewed[1] * inverse_depth + 0.5 * IMG_H
    slope_x = focal_len * viewed[0] * inverse_depth * inverse_depth
    slope_y = focal_len * viewed[1] * inverse_depth * inverse_depth
    jac_w = [
        [
            focal_len * inverse_depth * matrix[0][col_at] - slope_x * matrix[2][col_at]
            for col_at in range(3)
        ],
        [
            focal_len * inverse_depth * matrix[1][col_at] - slope_y * matrix[2][col_at]
            for col_at in range(3)
        ],
    ]
    quat_len = jnp.sqrt(
        values[6] * values[6]
        + values[7] * values[7]
        + values[8] * values[8]
        + values[9] * values[9]
    )
    quat_w = values[6] / quat_len
    quat_x = values[7] / quat_len
    quat_y = values[8] / quat_len
    quat_z = values[9] / quat_len
    rotation = [
        [
            1.0 - 2.0 * (quat_y * quat_y + quat_z * quat_z),
            2.0 * (quat_x * quat_y - quat_w * quat_z),
            2.0 * (quat_x * quat_z + quat_w * quat_y),
        ],
        [
            2.0 * (quat_x * quat_y + quat_w * quat_z),
            1.0 - 2.0 * (quat_x * quat_x + quat_z * quat_z),
            2.0 * (quat_y * quat_z - quat_w * quat_x),
        ],
        [
            2.0 * (quat_x * quat_z - quat_w * quat_y),
            2.0 * (quat_y * quat_z + quat_w * quat_x),
            1.0 - 2.0 * (quat_x * quat_x + quat_y * quat_y),
        ],
    ]
    extent = [jnp.exp(values[3]), jnp.exp(values[4]), jnp.exp(values[5])]
    spread = [
        [
            (
                jac_w[row_at][0] * rotation[0][col_at]
                + jac_w[row_at][1] * rotation[1][col_at]
                + jac_w[row_at][2] * rotation[2][col_at]
            )
            * extent[col_at]
            for col_at in range(3)
        ]
        for row_at in range(2)
    ]
    cov_a = (
        spread[0][0] * spread[0][0]
        + spread[0][1] * spread[0][1]
        + spread[0][2] * spread[0][2]
        + blur_add
    )
    cov_b = spread[0][0] * spread[1][0] + spread[0][1] * spread[1][1] + spread[0][2] * spread[1][2]
    cov_c = (
        spread[1][0] * spread[1][0]
        + spread[1][1] * spread[1][1]
        + spread[1][2] * spread[1][2]
        + blur_add
    )
    determinant = cov_a * cov_c - cov_b * cov_b
    opacity = jax.nn.sigmoid(values[10])
    center = [
        -(
            matrix[0][col_at] * translation[0]
            + matrix[1][col_at] * translation[1]
            + matrix[2][col_at] * translation[2]
        )
        for col_at in range(3)
    ]
    offset = [points[col_at] - center[col_at] for col_at in range(3)]
    distance = jnp.sqrt(offset[0] * offset[0] + offset[1] * offset[1] + offset[2] * offset[2])
    colors = sh_color(values, offset[0] / distance, offset[1] / distance, offset[2] / distance)
    first_rows = jnp.stack(
        [
            screen_x,
            screen_y,
            cov_c / determinant,
            -cov_b / determinant,
            cov_a / determinant,
            opacity,
        ]
    )
    return jnp.concatenate([first_rows, colors], axis=0)


def render_blocks(proj_rows, live_mask, pix_x, pix_y):
    nblocks = proj_rows.shape[1] // BLOCK
    grouped = proj_rows.reshape(proj_rows.shape[0], nblocks, BLOCK).transpose(1, 0, 2)
    block_masks = live_mask.reshape(nblocks, BLOCK)

    def block_step(carried, block_item):
        log_level, painted = carried
        block_rows, block_mask = block_item
        off_x = pix_x[None, :] - block_rows[0][:, None]
        off_y = pix_y[None, :] - block_rows[1][:, None]
        exponent = (
            -0.5 * (block_rows[2][:, None] * off_x * off_x + block_rows[4][:, None] * off_y * off_y)
            - block_rows[3][:, None] * off_x * off_y
        )
        alpha_px = (block_rows[5] * block_mask)[:, None] * jnp.exp(exponent)
        fade_log = jnp.log1p(-alpha_px)
        running = jnp.cumsum(fade_log, axis=0)
        weights = alpha_px * jnp.exp(log_level[None, :] + running - fade_log)
        painted = painted + jnp.dot(block_rows[6:9], weights, precision=lax.Precision.HIGHEST)
        return ((log_level + running[-1], painted), None)

    initial = (jnp.zeros(pix_x.shape, jnp.float32), jnp.zeros((3, pix_x.shape[0]), jnp.float32))
    (log_level, painted), unused = lax.scan(block_step, initial, (grouped, block_masks))
    return painted


def body(
    params,
    adam_m,
    adam_v,
    cameras,
    exposure,
    entry_owner,
    entry_local,
    block_counts,
    tile_view,
    tile_spot,
    d_image,
):
    devices = lax.axis_size(("tiles", "gauss"))
    gauss_dev = params.shape[1]
    tile_dev, slot_count = entry_owner.shape
    entries = tile_dev * slot_count
    capacity = 3 * entries // (2 * devices)
    owners = entry_owner.reshape(entries)
    request = jnp.repeat(tile_view, slot_count) * gauss_dev + entry_local.reshape(entries)
    sort_order = jnp.argsort(owners, stable=True)
    sorted_owner = owners[sort_order]
    starts = jnp.searchsorted(sorted_owner, jnp.arange(devices, dtype=jnp.int32), side="left")
    ranked = jnp.arange(entries, dtype=jnp.int32) - starts[sorted_owner]
    target = jnp.zeros((entries,), jnp.int32).at[sort_order].set(sorted_owner * capacity + ranked)
    outgoing = jnp.full((devices * capacity,), -1, jnp.int32).at[target].set(request)
    incoming = lax.all_to_all(outgoing, ("tiles", "gauss"), split_axis=0, concat_axis=0, tiled=True)
    present = incoming >= 0
    across = IMG_W // TILE
    pixel_ids = jnp.arange(TPIX, dtype=jnp.int32)
    pix_x = ((tile_spot % across)[:, None] * TILE + pixel_ids[None, :] % TILE).astype(
        jnp.float32
    ) + 0.5
    pix_y = ((tile_spot // across)[:, None] * TILE + pixel_ids[None, :] // TILE).astype(
        jnp.float32
    ) + 0.5
    live_mask = (
        (jnp.arange(slot_count, dtype=jnp.int32) // BLOCK)[None, :] < block_counts[:, None]
    ).astype(jnp.float32)
    picker = (tile_view[:, None] == jnp.arange(VIEWS, dtype=jnp.int32)[None, :]).astype(jnp.float32)
    tile_gains = jnp.dot(picker, exposure, precision=lax.Precision.HIGHEST)
    tile_cameras = jnp.dot(picker, cameras, precision=lax.Precision.HIGHEST)
    replies = jnp.take(params, jnp.maximum(incoming, 0) % gauss_dev, axis=1)
    arrived = lax.all_to_all(replies, ("tiles", "gauss"), split_axis=1, concat_axis=1, tiled=True)
    entry_rows = (
        jnp.take(arrived, target, axis=1).reshape(PARAMS, tile_dev, slot_count).transpose(1, 0, 2)
    )

    def tile_grad(tile_item):
        row_block, camera_row, mask_row, x_row, y_row, gain_vec, cotangent = tile_item

        def tile_image(rows_in, gains_in):
            return gains_in[:, None] * render_blocks(
                project(rows_in, camera_row[:, None]), mask_row, x_row, y_row
            )

        rendered, pullback = jax.vjp(tile_image, row_block, gain_vec)
        return pullback(cotangent)

    grad_rows, grad_gains = lax.map(
        tile_grad, (entry_rows, tile_cameras, live_mask, pix_x, pix_y, tile_gains, d_image)
    )
    entry_grads = grad_rows.transpose(1, 0, 2).reshape(PARAMS, entries)
    outgoing_grads = (
        jnp.zeros((PARAMS, devices * capacity), jnp.float32).at[:, target].set(entry_grads)
    )
    returned = lax.all_to_all(
        outgoing_grads, ("tiles", "gauss"), split_axis=1, concat_axis=1, tiled=True
    )
    local_index = jnp.where(present, incoming % gauss_dev, gauss_dev)
    gradient = (
        jnp.zeros((PARAMS, gauss_dev + 1), jnp.float32).at[:, local_index].add(returned)[:, :-1]
    )
    expo_local = jnp.dot(picker.T, grad_gains, precision=lax.Precision.HIGHEST)
    exposure_grad = lax.psum(expo_local, ("tiles", "gauss")) / devices
    new_m = beta_first * adam_m + (1.0 - beta_first) * gradient
    new_v = beta_second * adam_v + (1.0 - beta_second) * gradient * gradient
    new_params = params - learn_rate * (new_m / fix_first) / (
        jnp.sqrt(new_v / fix_second) + adam_eps
    )
    return (new_params, new_m, new_v, exposure_grad)


def solution(mesh):
    placed = (
        P(None, ("tiles", "gauss")),
        P(None, ("tiles", "gauss")),
        P(None, ("tiles", "gauss")),
        P(),
        P(),
        P(("tiles", "gauss"), None),
        P(("tiles", "gauss"), None),
        P(("tiles", "gauss")),
        P(("tiles", "gauss")),
        P(("tiles", "gauss")),
        P(("tiles", "gauss"), None, None),
    )
    return jax.shard_map(
        body,
        mesh=mesh,
        in_specs=placed,
        out_specs=(
            P(None, ("tiles", "gauss")),
            P(None, ("tiles", "gauss")),
            P(None, ("tiles", "gauss")),
            P(),
        ),
        check_vma=False,
    )
```

profile of v0, /device:TPU:1, one launch (start us, length us, event | category | flops | bytes accessed | tf_op | source)
XLA Modules:
  0.0 854.1 jit_solution(9691868540588589673)
XLA Ops:
  1.4 5.8 sort.17
  7.2 23.0 %gather_fusion.1 = s32[4096]{0:T(1024)S(1)} fusion(s32[4096]{0:T(1024)S(1)} %bitcast.1032, s32[4096]{0:T(1024)S(1)} %get-tuple-element.1639), kind=kCustom, calls=%fused_computation.1 | custom fusion | bytes 49152 | tf_op jit(solution)/shard_map/gather | solution.py:221
  30.2 15.8 %while.148 = (s32[]{:T(128)}, u32[128]{0:T(128)S(1)}, u32[128]{0:T(128)S(1)}, s32[4096]{0:T(1024)S(1)}, s32[]{:T(128)}, /*index=5*/s32[]{:T(128)}, s32[]{}) while((s32[]{:T(128)}, u32[128]{0:T(128)S(1)}, u32[128]{0:T(128)S(1)}, s32[4096]{0:T(1024)S(1)}, s32[]{:T(128)}, /*index=5*/s32[]{:T(128)}, s32[]{}) %tuple.508), condition=%wide.region_2.3_spmd.clone, body=%wide.region_1.2_spmd.clone.sunk | while | flops 2692 | bytes 10340 | solution.py:222
  46.1 24.7 %gather_fusion.2 = s32[4096]{0:T(1024)S(1)} fusion(s32[128]{0:T(128)S(1)} %convert_element_type.20, s32[4096]{0:T(1024)S(1)} %broadcast_clamp_fusion.2), kind=kCustom, calls=%fused_computation.2 | custom fusion | bytes 49152 | tf_op jit(solution)/shard_map/gather | solution.py:223
  70.8 15.5 %scatter_custom_fusion = s32[4096]{0:T(1024)S(1)} fusion(s32[4096]{0:T(1024)S(1)} %get-tuple-element.1640, s32[4096]{0:T(1024)S(1)} %subtract_add_fusion, s32[]{:T(128)} %constant.484.clone.1), kind=kCustom, calls=%fused_computation.596 | custom fusion | bytes 16388 | tf_op jit(solution)/shard_map/scatter | solution.py:224
  86.5 15.5 %scatter_custom_fusion.1 = s32[6144]{0:T(1024)S(1)} fusion(s32[4096]{0:T(1024)S(1)} %get-tuple-element.1638, s32[4096]{0:T(1024)S(1)} %bitcast.1134, s32[]{:T(128)} %constant.483.clone.1), kind=kCustom, calls=%fused_computation.588 | custom fusion | bytes 24580 | tf_op jit(solution)/shard_map/scatter | solution.py:225
  102.8 11.5 %all-to-all-start = ((s32[128,48,1]{1,2,0:T(1,128)}), s32[128,48,1]{1,2,0:T(1,128)S(1)}, u32[]{:S(2)}, u32[]{:S(2)}) async-start(s32[128,48,1]{1,2,0:T(1,128)} %bitcast.81), calls=%async_computation | async-start | bytes 131072 | tf_op jit(solution)/shard_map/all_to_all | solution.py:226
  114.3 7.0 copy.134
  125.3 24.5 %gather_fusion.3 = f32[6144,59]{1,0:T(8,128)} fusion(f32[59,16384]{0,1:T(8,128)} %copy.134, s32[6144]{0:T(1024)S(1)} %broadcast_clamp_fusion), kind=kCustom, calls=%fused_computation.3 | custom fusion | bytes 2924544 | tf_op jit(solution)/shard_map/jit(_take)/gather | solution.py:242
  153.0 5.5 reshape.9949
  158.5 19.7 %all-to-all-start.1 = ((f32[128,1,2832]{2,1,0:T(1,128)}), f32[128,1,2832]{2,1,0:T(1,128)S(1)}, u32[]{:S(2)}, u32[]{:S(2)}) async-start(f32[128,1,2832]{2,1,0:T(1,128)} %reshape.9949), calls=%async_computation.1 | async-start | bytes 3014656 | tf_op jit(solution)/shard_map/all_to_all | solution.py:243
  178.7 23.3 %all-to-all-done.1 = f32[128,1,2832]{2,1,0:T(1,128)S(1)} async-done(((f32[128,1,2832]{2,1,0:T(1,128)}), f32[128,1,2832]{2,1,0:T(1,128)S(1)}, u32[]{:S(2)}, u32[]{:S(2)}) %all-to-all-start.1) | async-done | bytes 1450016 | tf_op jit(solution)/shard_map/all_to_all | solution.py:243
  202.6 5.9 reduce.72
  212.1 14.2 %gather_fusion.4 = f32[4096,59]{1,0:T(8,128)} fusion(f32[59,6144]{0,1:T(8,128)S(1)} %bitcast.1042, s32[4096]{0:T(1024)S(1)} %get-tuple-element.1637), kind=kCustom, calls=%fused_computation.4 | custom fusion | bytes 1949696 | tf_op jit(solution)/shard_map/jit(_take)/gather | solution.py:245
  229.6 451.8 %while.147 = (s32[]{:T(128)}, f32[4,59,1024]{2,1,0:T(8,128)}, f32[4,3]{1,0:T(4,128)S(1)}, f32[4,59,1024]{2,1,0:T(8,128)}, f32[4,13]{1,0:T(4,128)S(1)}, /*index=5...) while((s32[]{:T(128)}, f32[4,59,1024]{2,1,0:T(8,128)}, ...), condition=%wide.region_37.38_spmd, body=%wide.region_5.37_spmd.sunk | while | flops 33596216 | bytes 15937833 | solution.py:259
  244.2 9.8 %fusion.236 = (f32[1024]{0:T(1024)S(1)}, f32[1,1,1024]{2,1,0:T(1,128)S(1)}, f32[1024]{0:T(1024)S(1)}, f32[1,1,1024]{2,1,0:T(1,128)S(1)}, f32[1,1,1024]{2,1,0:T(1...) fusion(f32[]{:T(128)} %broadcast.13728, f32[]{:T(128)} %bitcast.945, ...), kind=kLoop, calls=%fused_computation.632.clone.1 | loop fusion | flops 21504 | bytes 41028 | tf_op jit(solution)/shard_map/while/body/eval_jaxpr/jvp()/mul | solution.py:82
  254.0 4.5 add_multiply_fusion.38
  258.6 4.4 add_multiply_fusion.39
  265.0 20.0 %while.149 = (s32[]{:T(128)}, f32[256]{0:T(256)S(1)}, f32[3,256]{1,0:T(4,128)S(1)}, f32[4,256,256]{2,1,0:T(8,128)}, f32[4,256,1]{1,2,0:T(1,128)S(1)}, /*index=5*...) while((s32[]{:T(128)}, f32[256]{0:T(256)S(1)}, ...), condition=%wide.region_9.9_spmd.clone, body=%wide.region_6.8_spmd.clone.sunk | while | flops 14749193 | bytes 4594060 | solution.py:196
  285.9 32.6 %while.150 = (s32[]{:T(128)}, f32[256]{0:T(256)S(1)}, f32[4,9,256]{2,1,0:T(8,128)S(1)}, f32[4,256,256]{2,1,0:T(8,128)}, f32[4,3,256]{2,1,0:T(4,128)S(1)}, /*inde...) while((s32[]{:T(128)}, f32[256]{0:T(256)S(1)}, ...), condition=%wide.region_20.20_spmd.clone, body=%wide.region_10.19_spmd.clone.sunk | while | flops 15546372 | bytes 6922508 | solution.py:196
  318.8 7.5 negate_add_fusion.2
  331.2 6.5 multiply_add_fusion.54
  357.2 9.8 %fusion.236 = (f32[1024]{0:T(1024)S(1)}, f32[1,1,1024]{2,1,0:T(1,128)S(1)}, f32[1024]{0:T(1024)S(1)}, f32[1,1,1024]{2,1,0:T(1,128)S(1)}, f32[1,1,1024]{2,1,0:T(1...) fusion(f32[]{:T(128)} %broadcast.13728, f32[]{:T(128)} %bitcast.945, ...), kind=kLoop, calls=%fused_computation.632.clone.1 | loop fusion | flops 21504 | bytes 41028 | tf_op jit(solution)/shard_map/while/body/eval_jaxpr/jvp()/mul | solution.py:82
  367.0 4.5 add_multiply_fusion.38
  378.1 20.0 %while.149 = (s32[]{:T(128)}, f32[256]{0:T(256)S(1)}, f32[3,256]{1,0:T(4,128)S(1)}, f32[4,256,256]{2,1,0:T(8,128)}, f32[4,256,1]{1,2,0:T(1,128)S(1)}, /*index=5*...) while((s32[]{:T(128)}, f32[256]{0:T(256)S(1)}, ...), condition=%wide.region_9.9_spmd.clone, body=%wide.region_6.8_spmd.clone.sunk | while | flops 14749193 | bytes 4594060 | solution.py:196
  398.9 32.6 %while.150 = (s32[]{:T(128)}, f32[256]{0:T(256)S(1)}, f32[4,9,256]{2,1,0:T(8,128)S(1)}, f32[4,256,256]{2,1,0:T(8,128)}, f32[4,3,256]{2,1,0:T(4,128)S(1)}, /*inde...) while((s32[]{:T(128)}, f32[256]{0:T(256)S(1)}, ...), condition=%wide.region_20.20_spmd.clone, body=%wide.region_10.19_spmd.clone.sunk | while | flops 15546372 | bytes 6922508 | solution.py:196
  431.9 7.5 negate_add_fusion.2
  444.2 6.5 multiply_add_fusion.54
  470.2 9.8 %fusion.236 = (f32[1024]{0:T(1024)S(1)}, f32[1,1,1024]{2,1,0:T(1,128)S(1)}, f32[1024]{0:T(1024)S(1)}, f32[1,1,1024]{2,1,0:T(1,128)S(1)}, f32[1,1,1024]{2,1,0:T(1...) fusion(f32[]{:T(128)} %broadcast.13728, f32[]{:T(128)} %bitcast.945, ...), kind=kLoop, calls=%fused_computation.632.clone.1 | loop fusion | flops 21504 | bytes 41028 | tf_op jit(solution)/shard_map/while/body/eval_jaxpr/jvp()/mul | solution.py:82
  480.0 4.5 add_multiply_fusion.38
  491.0 20.0 %while.149 = (s32[]{:T(128)}, f32[256]{0:T(256)S(1)}, f32[3,256]{1,0:T(4,128)S(1)}, f32[4,256,256]{2,1,0:T(8,128)}, f32[4,256,1]{1,2,0:T(1,128)S(1)}, /*index=5*...) while((s32[]{:T(128)}, f32[256]{0:T(256)S(1)}, ...), condition=%wide.region_9.9_spmd.clone, body=%wide.region_6.8_spmd.clone.sunk | while | flops 14749193 | bytes 4594060 | solution.py:196
  511.8 32.6 %while.150 = (s32[]{:T(128)}, f32[256]{0:T(256)S(1)}, f32[4,9,256]{2,1,0:T(8,128)S(1)}, f32[4,256,256]{2,1,0:T(8,128)}, f32[4,3,256]{2,1,0:T(4,128)S(1)}, /*inde...) while((s32[]{:T(128)}, f32[256]{0:T(256)S(1)}, ...), condition=%wide.region_20.20_spmd.clone, body=%wide.region_10.19_spmd.clone.sunk | while | flops 15546372 | bytes 6922508 | solution.py:196
  544.8 7.5 negate_add_fusion.2
  557.1 6.5 multiply_add_fusion.54
  583.1 9.8 %fusion.236 = (f32[1024]{0:T(1024)S(1)}, f32[1,1,1024]{2,1,0:T(1,128)S(1)}, f32[1024]{0:T(1024)S(1)}, f32[1,1,1024]{2,1,0:T(1,128)S(1)}, f32[1,1,1024]{2,1,0:T(1...) fusion(f32[]{:T(128)} %broadcast.13728, f32[]{:T(128)} %bitcast.945, ...), kind=kLoop, calls=%fused_computation.632.clone.1 | loop fusion | flops 21504 | bytes 41028 | tf_op jit(solution)/shard_map/while/body/eval_jaxpr/jvp()/mul | solution.py:82
  592.8 4.5 add_multiply_fusion.38
  603.9 20.0 %while.149 = (s32[]{:T(128)}, f32[256]{0:T(256)S(1)}, f32[3,256]{1,0:T(4,128)S(1)}, f32[4,256,256]{2,1,0:T(8,128)}, f32[4,256,1]{1,2,0:T(1,128)S(1)}, /*index=5*...) while((s32[]{:T(128)}, f32[256]{0:T(256)S(1)}, ...), condition=%wide.region_9.9_spmd.clone, body=%wide.region_6.8_spmd.clone.sunk | while | flops 14749193 | bytes 4594060 | solution.py:196
  624.8 32.6 %while.150 = (s32[]{:T(128)}, f32[256]{0:T(256)S(1)}, f32[4,9,256]{2,1,0:T(8,128)S(1)}, f32[4,256,256]{2,1,0:T(8,128)}, f32[4,3,256]{2,1,0:T(4,128)S(1)}, /*inde...) while((s32[]{:T(128)}, f32[256]{0:T(256)S(1)}, ...), condition=%wide.region_20.20_spmd.clone, body=%wide.region_10.19_spmd.clone.sunk | while | flops 15546372 | bytes 6922508 | solution.py:196
  657.7 7.5 negate_add_fusion.2
  670.1 6.5 multiply_add_fusion.54
  686.1 11.9 %scatter_custom_fusion.2 = f32[59,6144]{0,1:T(8,128)S(1)} fusion(s32[4096]{0:T(1024)S(1)} %get-tuple-element.1638, f32[4096,59]{1,0:T(8,128)} %copy.139, f32[]{:T(128)} %constant.482.clone.1), kind=kCustom, calls=%fused_computation.563 | custom fusion | bytes 1450496 | tf_op jit(solution)/shard_map/scatter | solution.py:264
  697.9 5.5 reshape.9951
  703.4 4.7 all-to-all-start.2
  708.3 75.3 %psum.7 = f32[4,3]{0,1:T(4,128)S(1)} all-reduce(f32[4,3]{0,1:T(4,128)S(1)} %fusion.171), channel_id=1, replica_groups=mesh['tiles'=16,'gauss'=8] {'tiles','gauss'}, use_global_device_ids=true, to_apply=%region_40.41 | all-reduce | flops 12 | bytes 96 | tf_op jit(solution)/shard_map/psum | solution.py:274
  792.1 37.6 %scatter_custom_fusion.3 = f32[59,16385]{0,1:T(8,128)} fusion(s32[6144]{0:T(1024)S(1)} %bitcast.1132, f32[6144,59]{1,0:T(8,128)} %bitcast.1081, f32[]{:T(128)} %constant.482.clone.1), kind=kCustom, calls=%fused_computation.557 | custom fusion | flops 362496 | bytes 3867372 | tf_op jit(solution)/shard_map/scatter-add | solution.py:271
  829.7 5.7 slice.611
  835.4 6.8 copy.145
  842.2 11.6 %divide_subtract_fusion = (f32[59,16384]{1,0:T(8,128)}, f32[59,16384]{1,0:T(8,128)}, f32[59,16384]{1,0:T(8,128)}) fusion(f32[59,16384]{1,0:T(8,128)} %param.19, f32[59,16384]{1,0:T(8,128)} %copy.145, f32[59,16384]{1,0:T(8,128)} %param.20, f32[59,16384]{1,0:T(8,128)} %param.21), kind=kLoop, calls=%fused_computation.560 | loop fusion | flops 11599872 | bytes 27066368 | tf_op jit(solution)/shard_map/sub | solution.py:277
  (1189 shorter events, 329.7 us)
Async XLA Ops:
  0.6 177.8 %copy-start = (f32[4,13]{1,0:T(4,128)S(1)}, f32[4,13]{1,0:T(4,128)}, u32[]{:S(2)}) copy-start(f32[4,13]{1,0:T(4,128)} %param.22) | copy-start | bytes 628
  46.1 40.3 %copy-start.6 = (s32[4]{0:T(128)S(1)}, s32[4]{0:T(128)}, u32[]{:S(2)}) copy-start(s32[4]{0:T(128)} %param.27) | copy-start | bytes 52
  46.1 40.3 %copy-start.2 = (s32[4,1024]{1,0:T(4,128)S(1)}, s32[4,1024]{1,0:T(4,128)}, u32[]{:S(2)}) copy-start(s32[4,1024]{1,0:T(4,128)} %param.25) | copy-start | bytes 49156
  102.8 20.8 %all-to-all-start = ((s32[128,48,1]{1,2,0:T(1,128)}), s32[128,48,1]{1,2,0:T(1,128)S(1)}, u32[]{:S(2)}, u32[]{:S(2)}) async-start(s32[128,48,1]{1,2,0:T(1,128)} %bitcast.81), calls=%async_computation | async-start | bytes 131072 | tf_op jit(solution)/shard_map/all_to_all | solution.py:226
  153.0 25.2 %copy-start.5 = (s32[4]{0:T(128)S(1)}, s32[4]{0:T(128)}, u32[]{:S(2)}) copy-start(s32[4]{0:T(128)} %param.28) | copy-start | bytes 52
  153.0 25.2 %copy-start.4 = (f32[4,3]{1,0:T(4,128)S(1)}, f32[4,3]{1,0:T(4,128)}, u32[]{:S(2)}) copy-start(f32[4,3]{1,0:T(4,128)} %param.23) | copy-start | bytes 148
  153.0 25.7 %copy-start.3 = (s32[4]{0:T(128)S(1)}, s32[4]{0:T(128)}, u32[]{:S(2)}) copy-start(s32[4]{0:T(128)} %param.26) | copy-start | bytes 52
  158.5 43.6 %all-to-all-start.1 = ((f32[128,1,2832]{2,1,0:T(1,128)}), f32[128,1,2832]{2,1,0:T(1,128)S(1)}, u32[]{:S(2)}, u32[]{:S(2)}) async-start(f32[128,1,2832]{2,1,0:T(1,128)} %reshape.9949), calls=%async_computation.1 | async-start | bytes 3014656 | tf_op jit(solution)/shard_map/all_to_all | solution.py:243
  703.4 80.8 %all-to-all-start.2 = ((f32[128,1,2832]{2,1,0:T(1,128)}), f32[128,1,2832]{2,1,0:T(1,128)S(1)}, u32[]{:S(2)}, u32[]{:S(2)}) async-start(f32[128,1,2832]{2,1,0:T(1,128)} %reshape.9951), calls=%async_computation.2 | async-start | bytes 3014656 | tf_op jit(solution)/shard_map/all_to_all | solution.py:266
  842.2 11.6 %copy-start.1 = (f32[4,13]{1,0:T(4,128)S(1)}, f32[4,13]{1,0:T(4,128)}, u32[]{:S(2)}) copy-start(f32[4,13]{1,0:T(4,128)} %param.22) | copy-start | bytes 628
where the time goes:
time: 870 us; the launch traced here: 854 us
  other arithmetic  399 us (46%)
  local copies, waits for them, and re-layouts  215 us (25%)
  blocking collectives  75.3 us (9%)
  matrix products  51.3 us (6%)
  loops' own time  51 us (6%)
  starting transfers between devices  35.8 us (4%)
  waiting for transfers between devices  25.6 us (3%)
    psum x1, blocking collectives, body(): exposure_grad = lax.psum(expo_local, ('tiles', 'gauss')) / devices  75.3 us
    another operation x157, other arithmetic  53.4 us
    dot_general x48, matrix products, block_step(): jnp.dot(block_rows[6:9], weights, precision=lax.Precision.HIGHEST)  50.7 us
    another operation x1, loops' own time, body(): lax.map(tile_grad, (entry_rows, tile_cameras, live_mask, pix_x, pix_y, ti...  47.4 us
    dynamic_update_slice x64, other arithmetic, render_blocks(): lax.scan(block_step, initial, (grouped, block_masks))  43.3 us
    mul x4, other arithmetic, project(): screen_y = focal_len * viewed[1] * inverse_depth + 0.5 * IMG_H  39 us
    scatter-add x1, other arithmetic, body(): jnp.zeros((PARAMS, gauss_dev + 1), jnp.float32).at[:, local_index]  37.6 us
    mul x16, other arithmetic, project(): (jac_w[row_at][0] * rotation[0][col_at] + jac_w[row_at][1] * rotation[1][...  35.4 us
  transfers between devices with their start and end apart: 3, of which 2 were waited for; matrix products, arithmetic and copies ran while one was open for 1% of the time, Pallas kernels for 0%

commit v1 on v0

--- a/solution.py
+++ b/solution.py
@@ -1,3 +1,4 @@
+import functools
 import jax
 import jax.numpy as jnp
 from jax import lax
@@ -35,6 +36,14 @@
 fix_first = 1.0
 fix_second = 0.632304575229036
 blur_add = 0.3
+
+
+def zone_draft(x_part, mesh_ax):
+    s_next = jnp.sum(lax.all_gather(x_part, axis_name=mesh_ax), axis=0)
+    return s_next
+
+
+_make_lots_all = functools.partial(zone_draft, mesh_ax=("tiles", "gauss"))
 
 
 def sh_color(values, unit_x, unit_y, unit_z):
@@ -271,7 +280,7 @@
         jnp.zeros((PARAMS, gauss_dev + 1), jnp.float32).at[:, local_index].add(returned)[:, :-1]
     )
     expo_local = jnp.dot(picker.T, grad_gains, precision=lax.Precision.HIGHEST)
-    exposure_grad = lax.psum(expo_local, ("tiles", "gauss")) / devices
+    exposure_grad = _make_lots_all(expo_local) / devices
     new_m = beta_first * adam_m + (1.0 - beta_first) * gradient
     new_v = beta_second * adam_v + (1.0 - beta_second) * gradient * gradient
     new_params = params - learn_rate * (new_m / fix_first) / (

time: 870 us -> 843 us (0.969)
  blocking collectives: 75.3 us -> 48.7 us
    psum x1 -> x0, blocking collectives: 75.3 us -> none  [body(): exposure_grad = lax.psum(expo_local, ('tiles', 'gauss')) / devices]
    all_gather x0 -> x1, blocking collectives: none -> 48.7 us  [zone_draft(): s_next = jnp.sum(lax.all_gather(x_part, axis_name=mesh_ax), axis=0)]
    unnamed x25 -> x24, local copies, waits for them, and re-layouts: 34.2 us -> 33.7 us
where the time goes in v1:
time: 843 us; the launch traced here: 828 us
  other arithmetic  400 us (47%)
  local copies, waits for them, and re-layouts  214 us (25%)
  matrix products  51.4 us (6%)
  loops' own time  51 us (6%)
  blocking collectives  48.7 us (6%)
  starting transfers between devices  35.8 us (4%)
  waiting for transfers between devices  25.6 us (3%)
    another operation x157, other arithmetic  53.4 us
    dot_general x48, matrix products, block_step(): jnp.dot(block_rows[6:9], weights, precision=lax.Precision.HIGHEST)  50.7 us
    all_gather x1, blocking collectives, zone_draft(): s_next = jnp.sum(lax.all_gather(x_part, axis_name=mesh_ax), axis=0)  48.7 us
    another operation x1, loops' own time, body(): lax.map(tile_grad, (entry_rows, tile_cameras, live_mask, pix_x, pix_y, ti...  47.4 us
    dynamic_update_slice x64, other arithmetic, render_blocks(): lax.scan(block_step, initial, (grouped, block_masks))  43.3 us
    mul x4, other arithmetic, project(): screen_y = focal_len * viewed[1] * inverse_depth + 0.5 * IMG_H  39 us
    scatter-add x1, other arithmetic, body(): jnp.zeros((PARAMS, gauss_dev + 1), jnp.float32).at[:, local_index]  37.6 us
    mul x16, other arithmetic, project(): (jac_w[row_at][0] * rotation[0][col_at] + jac_w[row_at][1] * rotation[1][...  35.4 us
  transfers between devices with their start and end apart: 3, of which 2 were waited for; matrix products, arithmetic and copies ran while one was open for 1% of the time, Pallas kernels for 0%

profile of v1, /device:TPU:1, one launch (start us, length us, event | category | flops | bytes accessed | tf_op | source)
XLA Modules:
  0.0 828.0 jit_solution(4833168119230224413)
XLA Ops:
  1.4 5.8 sort.17
  7.2 23.0 %gather_fusion.1 = s32[4096]{0:T(1024)S(1)} fusion(s32[4096]{0:T(1024)S(1)} %bitcast.1034, s32[4096]{0:T(1024)S(1)} %get-tuple-element.1635), kind=kCustom, calls=%fused_computation.1 | custom fusion | bytes 49152 | tf_op jit(solution)/shard_map/gather | solution.py:230
  30.2 15.8 %while.148 = (s32[]{:T(128)}, u32[128]{0:T(128)S(1)}, u32[128]{0:T(128)S(1)}, s32[4096]{0:T(1024)S(1)}, s32[]{:T(128)}, /*index=5*/s32[]{:T(128)}, s32[]{}) while((s32[]{:T(128)}, u32[128]{0:T(128)S(1)}, u32[128]{0:T(128)S(1)}, s32[4096]{0:T(1024)S(1)}, s32[]{:T(128)}, /*index=5*/s32[]{:T(128)}, s32[]{}) %tuple.507), condition=%wide.region_2.3_spmd.clone, body=%wide.region_1.2_spmd.clone.sunk | while | flops 2692 | bytes 10340 | solution.py:231
  46.1 24.7 %gather_fusion.2 = s32[4096]{0:T(1024)S(1)} fusion(s32[128]{0:T(128)S(1)} %convert_element_type.20, s32[4096]{0:T(1024)S(1)} %broadcast_clamp_fusion.2), kind=kCustom, calls=%fused_computation.2 | custom fusion | bytes 49152 | tf_op jit(solution)/shard_map/gather | solution.py:232
  70.8 15.5 %scatter_custom_fusion = s32[4096]{0:T(1024)S(1)} fusion(s32[4096]{0:T(1024)S(1)} %get-tuple-element.1636, s32[4096]{0:T(1024)S(1)} %subtract_add_fusion, s32[]{:T(128)} %constant.485.clone.1), kind=kCustom, calls=%fused_computation.597 | custom fusion | bytes 16388 | tf_op jit(solution)/shard_map/scatter | solution.py:233
  86.5 15.5 %scatter_custom_fusion.1 = s32[6144]{0:T(1024)S(1)} fusion(s32[4096]{0:T(1024)S(1)} %get-tuple-element.1634, s32[4096]{0:T(1024)S(1)} %bitcast.1136, s32[]{:T(128)} %constant.484.clone.1), kind=kCustom, calls=%fused_computation.589 | custom fusion | bytes 24580 | tf_op jit(solution)/shard_map/scatter | solution.py:234
  102.8 11.5 %all-to-all-start = ((s32[128,48,1]{1,2,0:T(1,128)}), s32[128,48,1]{1,2,0:T(1,128)S(1)}, u32[]{:S(2)}, u32[]{:S(2)}) async-start(s32[128,48,1]{1,2,0:T(1,128)} %bitcast.81), calls=%async_computation | async-start | bytes 131072 | tf_op jit(solution)/shard_map/all_to_all | solution.py:235
  114.3 7.0 copy.134
  125.3 24.5 %gather_fusion.3 = f32[6144,59]{1,0:T(8,128)} fusion(f32[59,16384]{0,1:T(8,128)} %copy.134, s32[6144]{0:T(1024)S(1)} %broadcast_clamp_fusion), kind=kCustom, calls=%fused_computation.3 | custom fusion | bytes 2924544 | tf_op jit(solution)/shard_map/jit(_take)/gather | solution.py:251
  153.0 5.5 reshape.9953
  158.5 19.7 %all-to-all-start.1 = ((f32[128,1,2832]{2,1,0:T(1,128)}), f32[128,1,2832]{2,1,0:T(1,128)S(1)}, u32[]{:S(2)}, u32[]{:S(2)}) async-start(f32[128,1,2832]{2,1,0:T(1,128)} %reshape.9953), calls=%async_computation.1 | async-start | bytes 3014656 | tf_op jit(solution)/shard_map/all_to_all | solution.py:252
  178.7 23.3 %all-to-all-done.1 = f32[128,1,2832]{2,1,0:T(1,128)S(1)} async-done(((f32[128,1,2832]{2,1,0:T(1,128)}), f32[128,1,2832]{2,1,0:T(1,128)S(1)}, u32[]{:S(2)}, u32[]{:S(2)}) %all-to-all-start.1) | async-done | bytes 1450016 | tf_op jit(solution)/shard_map/all_to_all | solution.py:252
  202.6 5.9 reduce.73
  212.1 14.2 %gather_fusion.4 = f32[4096,59]{1,0:T(8,128)} fusion(f32[59,6144]{0,1:T(8,128)S(1)} %bitcast.1044, s32[4096]{0:T(1024)S(1)} %get-tuple-element.1633), kind=kCustom, calls=%fused_computation.4 | custom fusion | bytes 1949696 | tf_op jit(solution)/shard_map/jit(_take)/gather | solution.py:254
  229.6 451.8 %while.147 = (s32[]{:T(128)}, f32[4,59,1024]{2,1,0:T(8,128)}, f32[4,3]{1,0:T(4,128)S(1)}, f32[4,59,1024]{2,1,0:T(8,128)}, f32[4,13]{1,0:T(4,128)S(1)}, /*index=5...) while((s32[]{:T(128)}, f32[4,59,1024]{2,1,0:T(8,128)}, ...), condition=%wide.region_37.38_spmd, body=%wide.region_5.37_spmd.sunk | while | flops 33596216 | bytes 15937833 | solution.py:268
  244.2 9.8 %fusion.235 = (f32[1024]{0:T(1024)S(1)}, f32[1,1,1024]{2,1,0:T(1,128)S(1)}, f32[1024]{0:T(1024)S(1)}, f32[1,1,1024]{2,1,0:T(1,128)S(1)}, f32[1,1,1024]{2,1,0:T(1...) fusion(f32[]{:T(128)} %broadcast.13728, f32[]{:T(128)} %bitcast.947, ...), kind=kLoop, calls=%fused_computation.632.clone.1 | loop fusion | flops 21504 | bytes 41028 | tf_op jit(solution)/shard_map/while/body/eval_jaxpr/jvp()/mul | solution.py:91
  254.0 4.5 add_multiply_fusion.38
  265.0 20.0 %while.149 = (s32[]{:T(128)}, f32[256]{0:T(256)S(1)}, f32[3,256]{1,0:T(4,128)S(1)}, f32[4,256,256]{2,1,0:T(8,128)}, f32[4,256,1]{1,2,0:T(1,128)S(1)}, /*index=5*...) while((s32[]{:T(128)}, f32[256]{0:T(256)S(1)}, ...), condition=%wide.region_9.9_spmd.clone, body=%wide.region_6.8_spmd.clone.sunk | while | flops 14749193 | bytes 4594060 | solution.py:205
  285.9 32.6 %while.150 = (s32[]{:T(128)}, f32[256]{0:T(256)S(1)}, f32[4,9,256]{2,1,0:T(8,128)S(1)}, f32[4,256,256]{2,1,0:T(8,128)}, f32[4,3,256]{2,1,0:T(4,128)S(1)}, /*inde...) while((s32[]{:T(128)}, f32[256]{0:T(256)S(1)}, ...), condition=%wide.region_20.20_spmd.clone, body=%wide.region_10.19_spmd.clone.sunk | while | flops 15546372 | bytes 6922508 | solution.py:205
  318.8 7.5 negate_add_fusion.2
  331.2 6.5 multiply_add_fusion.54
  357.2 9.8 %fusion.235 = (f32[1024]{0:T(1024)S(1)}, f32[1,1,1024]{2,1,0:T(1,128)S(1)}, f32[1024]{0:T(1024)S(1)}, f32[1,1,1024]{2,1,0:T(1,128)S(1)}, f32[1,1,1024]{2,1,0:T(1...) fusion(f32[]{:T(128)} %broadcast.13728, f32[]{:T(128)} %bitcast.947, ...), kind=kLoop, calls=%fused_computation.632.clone.1 | loop fusion | flops 21504 | bytes 41028 | tf_op jit(solution)/shard_map/while/body/eval_jaxpr/jvp()/mul | solution.py:91
  367.0 4.5 add_multiply_fusion.38
  378.1 20.0 %while.149 = (s32[]{:T(128)}, f32[256]{0:T(256)S(1)}, f32[3,256]{1,0:T(4,128)S(1)}, f32[4,256,256]{2,1,0:T(8,128)}, f32[4,256,1]{1,2,0:T(1,128)S(1)}, /*index=5*...) while((s32[]{:T(128)}, f32[256]{0:T(256)S(1)}, ...), condition=%wide.region_9.9_spmd.clone, body=%wide.region_6.8_spmd.clone.sunk | while | flops 14749193 | bytes 4594060 | solution.py:205
  398.9 32.6 %while.150 = (s32[]{:T(128)}, f32[256]{0:T(256)S(1)}, f32[4,9,256]{2,1,0:T(8,128)S(1)}, f32[4,256,256]{2,1,0:T(8,128)}, f32[4,3,256]{2,1,0:T(4,128)S(1)}, /*inde...) while((s32[]{:T(128)}, f32[256]{0:T(256)S(1)}, ...), condition=%wide.region_20.20_spmd.clone, body=%wide.region_10.19_spmd.clone.sunk | while | flops 15546372 | bytes 6922508 | solution.py:205
  431.9 7.5 negate_add_fusion.2
  444.2 6.5 multiply_add_fusion.54
  470.2 9.8 %fusion.235 = (f32[1024]{0:T(1024)S(1)}, f32[1,1,1024]{2,1,0:T(1,128)S(1)}, f32[1024]{0:T(1024)S(1)}, f32[1,1,1024]{2,1,0:T(1,128)S(1)}, f32[1,1,1024]{2,1,0:T(1...) fusion(f32[]{:T(128)} %broadcast.13728, f32[]{:T(128)} %bitcast.947, ...), kind=kLoop, calls=%fused_computation.632.clone.1 | loop fusion | flops 21504 | bytes 41028 | tf_op jit(solution)/shard_map/while/body/eval_jaxpr/jvp()/mul | solution.py:91
  480.0 4.5 add_multiply_fusion.38
  491.0 20.0 %while.149 = (s32[]{:T(128)}, f32[256]{0:T(256)S(1)}, f32[3,256]{1,0:T(4,128)S(1)}, f32[4,256,256]{2,1,0:T(8,128)}, f32[4,256,1]{1,2,0:T(1,128)S(1)}, /*index=5*...) while((s32[]{:T(128)}, f32[256]{0:T(256)S(1)}, ...), condition=%wide.region_9.9_spmd.clone, body=%wide.region_6.8_spmd.clone.sunk | while | flops 14749193 | bytes 4594060 | solution.py:205
  511.8 32.6 %while.150 = (s32[]{:T(128)}, f32[256]{0:T(256)S(1)}, f32[4,9,256]{2,1,0:T(8,128)S(1)}, f32[4,256,256]{2,1,0:T(8,128)}, f32[4,3,256]{2,1,0:T(4,128)S(1)}, /*inde...) while((s32[]{:T(128)}, f32[256]{0:T(256)S(1)}, ...), condition=%wide.region_20.20_spmd.clone, body=%wide.region_10.19_spmd.clone.sunk | while | flops 15546372 | bytes 6922508 | solution.py:205
  544.8 7.5 negate_add_fusion.2
  557.1 6.5 multiply_add_fusion.54
  583.1 9.8 %fusion.235 = (f32[1024]{0:T(1024)S(1)}, f32[1,1,1024]{2,1,0:T(1,128)S(1)}, f32[1024]{0:T(1024)S(1)}, f32[1,1,1024]{2,1,0:T(1,128)S(1)}, f32[1,1,1024]{2,1,0:T(1...) fusion(f32[]{:T(128)} %broadcast.13728, f32[]{:T(128)} %bitcast.947, ...), kind=kLoop, calls=%fused_computation.632.clone.1 | loop fusion | flops 21504 | bytes 41028 | tf_op jit(solution)/shard_map/while/body/eval_jaxpr/jvp()/mul | solution.py:91
  592.8 4.5 add_multiply_fusion.38
  597.4 4.4 add_multiply_fusion.39
  603.9 20.0 %while.149 = (s32[]{:T(128)}, f32[256]{0:T(256)S(1)}, f32[3,256]{1,0:T(4,128)S(1)}, f32[4,256,256]{2,1,0:T(8,128)}, f32[4,256,1]{1,2,0:T(1,128)S(1)}, /*index=5*...) while((s32[]{:T(128)}, f32[256]{0:T(256)S(1)}, ...), condition=%wide.region_9.9_spmd.clone, body=%wide.region_6.8_spmd.clone.sunk | while | flops 14749193 | bytes 4594060 | solution.py:205
  624.8 32.6 %while.150 = (s32[]{:T(128)}, f32[256]{0:T(256)S(1)}, f32[4,9,256]{2,1,0:T(8,128)S(1)}, f32[4,256,256]{2,1,0:T(8,128)}, f32[4,3,256]{2,1,0:T(4,128)S(1)}, /*inde...) while((s32[]{:T(128)}, f32[256]{0:T(256)S(1)}, ...), condition=%wide.region_20.20_spmd.clone, body=%wide.region_10.19_spmd.clone.sunk | while | flops 15546372 | bytes 6922508 | solution.py:205
  657.7 7.5 negate_add_fusion.2
  670.1 6.5 multiply_add_fusion.54
  686.1 11.9 %scatter_custom_fusion.2 = f32[59,6144]{0,1:T(8,128)S(1)} fusion(s32[4096]{0:T(1024)S(1)} %get-tuple-element.1634, f32[4096,59]{1,0:T(8,128)} %copy.139, f32[]{:T(128)} %constant.483.clone.1), kind=kCustom, calls=%fused_computation.563 | custom fusion | bytes 1450496 | tf_op jit(solution)/shard_map/scatter | solution.py:273
  697.9 5.5 reshape.9955
  703.4 4.7 all-to-all-start.2
  708.3 48.7 %all-gather.1 = f32[128,4,3]{2,1,0:T(4,128)S(1)} all-gather(f32[1,4,3]{2,1,0:T(4,128)S(1)} %convolution_bitcast_fusion.1), channel_id=2, replica_groups=mesh['tiles'=16,'gauss'=8] {'tiles','gauss'}, dimensions={0}, use_global_device_ids=true | all-gather | bytes 6192 | tf_op jit(solution)/shard_map/all_gather | solution.py:42
  765.9 37.6 %scatter_custom_fusion.3 = f32[59,16385]{0,1:T(8,128)} fusion(s32[6144]{0:T(1024)S(1)} %bitcast.1134, f32[6144,59]{1,0:T(8,128)} %bitcast.1083, f32[]{:T(128)} %constant.483.clone.1), kind=kCustom, calls=%fused_computation.557 | custom fusion | flops 362496 | bytes 3867372 | tf_op jit(solution)/shard_map/scatter-add | solution.py:280
  803.5 5.7 slice.611
  809.2 6.8 copy.146
  816.0 11.6 %divide_subtract_fusion = (f32[59,16384]{1,0:T(8,128)}, f32[59,16384]{1,0:T(8,128)}, f32[59,16384]{1,0:T(8,128)}) fusion(f32[59,16384]{1,0:T(8,128)} %param.19, f32[59,16384]{1,0:T(8,128)} %copy.146, f32[59,16384]{1,0:T(8,128)} %param.20, f32[59,16384]{1,0:T(8,128)} %param.21), kind=kLoop, calls=%fused_computation.560 | loop fusion | flops 11599872 | bytes 27066368 | tf_op jit(solution)/shard_map/sub | solution.py:286
  (1189 shorter events, 330.1 us)
Async XLA Ops:
  0.6 177.8 %copy-start = (f32[4,13]{1,0:T(4,128)S(1)}, f32[4,13]{1,0:T(4,128)}, u32[]{:S(2)}) copy-start(f32[4,13]{1,0:T(4,128)} %param.22) | copy-start | bytes 628
  46.1 40.3 %copy-start.6 = (s32[4]{0:T(128)S(1)}, s32[4]{0:T(128)}, u32[]{:S(2)}) copy-start(s32[4]{0:T(128)} %param.27) | copy-start | bytes 52
  46.1 40.3 %copy-start.2 = (s32[4,1024]{1,0:T(4,128)S(1)}, s32[4,1024]{1,0:T(4,128)}, u32[]{:S(2)}) copy-start(s32[4,1024]{1,0:T(4,128)} %param.25) | copy-start | bytes 49156
  102.8 20.8 %all-to-all-start = ((s32[128,48,1]{1,2,0:T(1,128)}), s32[128,48,1]{1,2,0:T(1,128)S(1)}, u32[]{:S(2)}, u32[]{:S(2)}) async-start(s32[128,48,1]{1,2,0:T(1,128)} %bitcast.81), calls=%async_computation | async-start | bytes 131072 | tf_op jit(solution)/shard_map/all_to_all | solution.py:235
  153.0 25.2 %copy-start.5 = (s32[4]{0:T(128)S(1)}, s32[4]{0:T(128)}, u32[]{:S(2)}) copy-start(s32[4]{0:T(128)} %param.28) | copy-start | bytes 52
  153.0 25.2 %copy-start.4 = (f32[4,3]{1,0:T(4,128)S(1)}, f32[4,3]{1,0:T(4,128)}, u32[]{:S(2)}) copy-start(f32[4,3]{1,0:T(4,128)} %param.23) | copy-start | bytes 148
  153.0 25.7 %copy-start.3 = (s32[4]{0:T(128)S(1)}, s32[4]{0:T(128)}, u32[]{:S(2)}) copy-start(s32[4]{0:T(128)} %param.26) | copy-start | bytes 52
  158.5 43.6 %all-to-all-start.1 = ((f32[128,1,2832]{2,1,0:T(1,128)}), f32[128,1,2832]{2,1,0:T(1,128)S(1)}, u32[]{:S(2)}, u32[]{:S(2)}) async-start(f32[128,1,2832]{2,1,0:T(1,128)} %reshape.9953), calls=%async_computation.1 | async-start | bytes 3014656 | tf_op jit(solution)/shard_map/all_to_all | solution.py:252
  703.4 54.4 %all-to-all-start.2 = ((f32[128,1,2832]{2,1,0:T(1,128)}), f32[128,1,2832]{2,1,0:T(1,128)S(1)}, u32[]{:S(2)}, u32[]{:S(2)}) async-start(f32[128,1,2832]{2,1,0:T(1,128)} %reshape.9955), calls=%async_computation.2 | async-start | bytes 3014656 | tf_op jit(solution)/shard_map/all_to_all | solution.py:275
  816.0 11.6 %copy-start.1 = (f32[4,13]{1,0:T(4,128)S(1)}, f32[4,13]{1,0:T(4,128)}, u32[]{:S(2)}) copy-start(f32[4,13]{1,0:T(4,128)} %param.22) | copy-start | bytes 628
